TPU v7x, 256 devices: a whole 4x4x8 slice. The times are simulated.
256 devices in a mesh: slab: 8 (over z), filt: 32 (over y, x, core).
Axes of the slice: x: 4, y: 4, z: 8, core: 2. Of those that a mesh axis runs over, the one named last changes fastest.
Arguments:
- features: bfloat16 [32, 256, 64, 128], P('slab', 'filt'), may hold values from -6 to 6
- kernel: bfloat16 [3, 3, 3, 256, 256], P(None, None, None, 'filt'), may hold values from -0.078125 to 0.078125
- bias_vector: float32 [256], replicated, may hold values from -0.6 to 0.6
Outputs:
- activated: bfloat16 [32, 256, 64, 128], P('slab', 'filt')
All inputs are finite; a program needn't handle non-finite values.
Results may differ from a plain program's by a relative error of at most 0.005.
Values may be sent and summed in bfloat16 or wider, within the bound.
A program may use at most 128 MiB of HBM per device.

v0:
```python
import jax
import jax.numpy as jnp
from jax import lax
from jax.sharding import PartitionSpec as P

slope = 0.3


def with_halo(array, sides, width):
    for axis, dim in sides:
        devices, length = (lax.axis_size(axis), array.shape[dim])
        up = [(i, (i + 1) % devices) for i in range(devices - 1)]
        down = [(j, i) for i, j in up]
        last = lax.slice_in_dim(array, length - width, length, axis=dim)
        leading = lax.slice_in_dim(array, 0, width, axis=dim)
        before = lax.ppermute(last, axis, up)
        after = lax.ppermute(leading, axis, down)
        array = jnp.concatenate([before, array, after], axis=dim)
    return array


def convolve(volume_piece, taps, y_margin, first_center, out_count):
    in_planes, in_chan, in_rows, in_cols = volume_piece.shape
    out_chan = taps.shape[3]
    out_rows = in_rows - 2 * y_margin
    totals = [
        jnp.zeros((out_chan, out_rows, in_cols), jnp.float32) for slot_index in range(out_count)
    ]
    for plane_index in range(in_planes):
        depth_list = [
            plane_index - (first_center + slot_index) + 1 for slot_index in range(out_count)
        ]
        depth_list = [entry for entry in depth_list if 0 <= entry <= 2]
        depth_low = min(depth_list)
        depth_high = max(depth_list)
        depth_count = depth_high - depth_low + 1
        flat_weight = taps[depth_low : depth_high + 1].reshape(depth_count * 9 * out_chan, in_chan)
        products = jnp.einsum(
            "tc,cyx->tyx",
            flat_weight,
            volume_piece[plane_index],
            preferred_element_type=jnp.float32,
        )
        products = products.reshape(depth_count, 3, 3, out_chan, in_rows, in_cols)
        padded_products = jnp.pad(products, ((0, 0), (0, 0), (0, 0), (0, 0), (1, 1), (1, 1)))
        for slot_index in range(out_count):
            depth_tap = plane_index - (first_center + slot_index) + 1
            if 0 <= depth_tap <= 2:
                for row_tap in range(3):
                    for col_tap in range(3):
                        row_start = y_margin + row_tap
                        totals[slot_index] = (
                            totals[slot_index]
                            + padded_products[
                                depth_tap - depth_low,
                                row_tap,
                                col_tap,
                                :,
                                row_start : row_start + out_rows,
                                col_tap : col_tap + in_cols,
                            ]
                        )
    return jnp.stack(totals)


def finish(convolved, bias_piece):
    shifted = convolved + bias_piece[None, :, None, None]
    return jnp.where(shifted > 0, shifted, slope * shifted).astype(jnp.bfloat16)


def body(features, kernel, bias_vector):
    planes = features.shape[0]
    own_count = kernel.shape[3]
    own_bias = lax.dynamic_slice_in_dim(
        bias_vector, lax.axis_index("filt") * own_count, own_count, 0
    )
    padded = with_halo(features, (("slab", 0),), 1)
    gathered = lax.all_gather(padded, "filt", axis=1, tiled=True)
    convolved = convolve(gathered, kernel, 0, 1, planes)
    return finish(convolved, own_bias)


def solution(mesh):
    placed = (P("slab", "filt", None, None), P(None, None, None, "filt", None), P())
    return jax.shard_map(
        body, mesh=mesh, in_specs=placed, out_specs=P("slab", "filt", None, None), check_vma=False
    )
```

profile of v0, /device:TPU:1, one launch (start us, length us, event | category | flops | bytes accessed | tf_op | source)
XLA Modules:
  0.0 176.3 jit_solution(7436586387113536860)
XLA Ops:
  6.5 1.4 copy.4
  8.0 4.4 %collective-permute-start = (bf16[1,8,64,128]{3,1,2,0:T(8,128)(2,1)S(1)}, bf16[1,8,64,128]{3,1,2,0:T(8,128)(2,1)S(1)}, u32[]{:S(2)}, u32[]{:S(2)}) collective-permute-start(bf16[1,8,64,128]{3,1,2,0:T(8,128)(2,1)S(1)} %get-tuple-element.8), channel_id=1, source_target_pairs={{0,32},{32,64},{64,96},{96,128},{128,160},{160,192},{192,224},{1,3... | collective-permute-start | bytes 393224 | tf_op jit(solution)/shard_map/ppermute | solution.py:16
  12.3 1.3 collective-permute-start.1
  13.6 0.8 collective-permute-done
  14.5 4.2 %collective-permute-done.1 = bf16[1,8,64,128]{3,1,2,0:T(8,128)(2,1)S(1)} collective-permute-done((bf16[1,8,64,128]{3,1,2,0:T(8,128)(2,1)S(1)}, bf16[1,8,64,128]{3,1,2,0:T(8,128)(2,1)S(1)}, u32[]{:S(2)}, u32[]{:S(2)}) %collective-permute-start.1) | collective-permute-done | bytes 131104 | tf_op jit(solution)/shard_map/ppermute | solution.py:17
  18.7 1.1 pad_maximum_fusion
  19.7 0.8 dynamic_slice.3
  20.5 0.8 fusion.148
  21.3 1.0 fusion.149
  22.3 109.8 %all-gather.2.cloned.1.call-done = bf16[6,256,64,128]{3,1,2,0:T(8,128)(2,1)} async-done(((bf16[6,8,64,128]{3,1,2,0:T(8,128)(2,1)}), bf16[6,256,64,128]{3,1,2,0:T(8,128)(2,1)}) %all-gather.2.cloned.1.call-update) | async-done | bytes 25165840 | tf_op jit(solution)/shard_map/all_gather | solution.py:78
  132.1 3.0 %fusion = f32[64,128,72]{1,2,0:T(8,128)S(1)} fusion(bf16[72,256,1]{1,0,2:T(8,128)(2,1)S(1)} %bitcast.394, bf16[6,256,64,128]{3,1,2,0:T(8,128)(2,1)} %all-gather.2.cloned.1.call-done), kind=kOutput, calls=%fused_computation.97 | convolution fusion | flops 301989888 | bytes 6590464 | tf_op jit(solution)/shard_map/tc,cyx->tyx/dot_general | solution.py:38
  135.5 3.0 %fusion.5 = f32[64,128,72]{1,2,0:T(8,128)S(1)} fusion(bf16[72,256,1]{1,0,2:T(8,128)(2,1)S(1)} %bitcast.393, bf16[6,256,64,128]{3,1,2,0:T(8,128)(2,1)} %all-gather.2.cloned.1.call-done), kind=kOutput, calls=%fused_computation.107 | convolution fusion | flops 301989888 | bytes 6590464 | tf_op jit(solution)/shard_map/tc,cyx->tyx/dot_general | solution.py:38
  138.6 1.8 %copy.7 = f32[1,3,3,8,64,128]{5,4,3,2,1,0:T(8,128)} copy(f32[1,3,3,8,64,128]{5,3,2,1,4,0:T(8,128)S(1)} %bitcast.388) | data formatting | bytes 4718592 | tf_op jit(solution)/shard_map/reshape | solution.py:44
  140.4 3.0 %fusion.1 = f32[64,128,144]{1,2,0:T(8,128)S(1)} fusion(bf16[144,256,1]{1,0,2:T(8,128)(2,1)S(1)} %bitcast.392, bf16[6,256,64,128]{3,1,2,0:T(8,128)(2,1)} %all-gather.2.cloned.1.call-done), kind=kOutput, calls=%fused_computation.99 | convolution fusion | flops 603979776 | bytes 8986624 | tf_op jit(solution)/shard_map/tc,cyx->tyx/dot_general | solution.py:38
  143.4 3.6 %copy.19 = f32[2,3,3,8,64,128]{5,4,3,2,1,0:T(8,128)} copy(f32[2,3,3,8,64,128]{5,3,2,1,0,4:T(8,128)S(1)} %bitcast.385) | data formatting | bytes 9437184 | tf_op jit(solution)/shard_map/reshape | solution.py:44
  147.0 3.0 %fusion.4 = f32[64,128,144]{1,2,0:T(8,128)S(1)} fusion(bf16[144,256,1]{1,0,2:T(8,128)(2,1)S(1)} %bitcast.391, bf16[6,256,64,128]{3,1,2,0:T(8,128)(2,1)} %all-gather.2.cloned.1.call-done), kind=kOutput, calls=%fused_computation.105 | convolution fusion | flops 603979776 | bytes 8986624 | tf_op jit(solution)/shard_map/tc,cyx->tyx/dot_general | solution.py:38
  150.0 1.4 copy.9
  151.4 3.3 %fusion.3 = f32[64,128,216]{1,2,0:T(8,128)S(1)} fusion(bf16[216,256,1]{1,0,2:T(8,128)(2,1)S(1)} %bitcast.389, bf16[6,256,64,128]{3,1,2,0:T(8,128)(2,1)} %all-gather.2.cloned.1.call-done), kind=kOutput, calls=%fused_computation.103 | convolution fusion | flops 905969664 | bytes 11382784 | tf_op jit(solution)/shard_map/tc,cyx->tyx/dot_general | solution.py:38
  154.7 1.3 copy.11
  156.0 3.3 %fusion.2 = f32[64,128,216]{1,2,0:T(8,128)S(1)} fusion(bf16[216,256,1]{1,0,2:T(8,128)(2,1)S(1)} %bitcast.390, bf16[6,256,64,128]{3,1,2,0:T(8,128)(2,1)} %all-gather.2.cloned.1.call-done), kind=kOutput, calls=%fused_computation.101 | convolution fusion | flops 905969664 | bytes 11382784 | tf_op jit(solution)/shard_map/tc,cyx->tyx/dot_general | solution.py:38
  159.3 1.3 copy.15
  160.7 3.3 %fusion.123 = f32[1,8,64,128]{3,2,1,0:T(8,128)S(1)} fusion(f32[3,3,3,8,64,128]{5,4,3,2,1,0:T(8,128)S(1)} %copy.11, f32[2,3,3,8,64,128]{5,4,3,2,1,0:T(8,128)S(1)} %copy.9, f32[1,3,3,8,64,128]{5,4,3,2,1,0:T(8,128)} %copy.7), kind=kLoop, calls=%fused_computation.228 | loop fusion | flops 1703936 | bytes 15204352 | tf_op jit(solution)/shard_map/add | solution.py:53
  164.0 4.4 %fusion.142 = (f32[1,8,64,128]{3,2,1,0:T(8,128)S(1)}, f32[1,8,64,128]{3,2,1,0:T(8,128)S(1)}, f32[1,8,64,128]{3,2,1,0:T(8,128)S(1)}) fusion(f32[3,3,3,8,64,128]{5,4,3,2,1,0:T(8,128)S(1)} %copy.15, f32[3,3,3,8,64,128]{5,4,3,2,1,0:T(8,128)S(1)} %copy.11, f32[2,3,3,8,64,128]{5,4,3,2,1,0:T(8,128)S(1)} %copy.9, f32[2,3,3,8,64,128]{5,4,3,2,1,0:T(8,128)S(1)} %bitcast.384, ...), kind=kLoop, calls=%fused_computation.247 | loop fusion | flops 5111808 | bytes 29097984 | tf_op jit(solution)/shard_map/add | solution.py:53
  168.4 1.0 fusion.6
  (11 shorter events, 0.5 us)
Async XLA Ops:
  6.5 125.6 %all-gather.2.cloned.1.call-start = ((), (), s32[]{:S(2)}) async-start(), calls=%async_computation | async-start | bytes 25952256 | tf_op jit(solution)/shard_map/all_gather | solution.py:78
  8.0 6.5 %collective-permute-start = (bf16[1,8,64,128]{3,1,2,0:T(8,128)(2,1)S(1)}, bf16[1,8,64,128]{3,1,2,0:T(8,128)(2,1)S(1)}, u32[]{:S(2)}, u32[]{:S(2)}) collective-permute-start(bf16[1,8,64,128]{3,1,2,0:T(8,128)(2,1)S(1)} %get-tuple-element.8), channel_id=1, source_target_pairs={{0,32},{32,64},{64,96},{96,128},{128,160},{160,192},{192,224},{1,3... | collective-permute-start | bytes 393224 | tf_op jit(solution)/shard_map/ppermute | solution.py:16
  12.3 6.3 %collective-permute-start.1 = (bf16[1,8,64,128]{3,1,2,0:T(8,128)(2,1)S(1)}, bf16[1,8,64,128]{3,1,2,0:T(8,128)(2,1)S(1)}, u32[]{:S(2)}, u32[]{:S(2)}) collective-permute-start(bf16[1,8,64,128]{3,1,2,0:T(8,128)(2,1)S(1)} %get-tuple-element.9), channel_id=1, source_target_pairs={{32,0},{64,32},{96,64},{128,96},{160,128},{192,160},{224,192},{33,... | collective-permute-start | bytes 393224 | tf_op jit(solution)/shard_map/ppermute | solution.py:17
  147.0 4.4 %copy-start = (bf16[3,3,3,8,256]{4,3,2,1,0:T(8,128)(2,1)S(1)}, bf16[3,3,3,8,256]{4,3,2,1,0:T(8,128)(2,1)}, u32[]{:S(2)}) copy-start(bf16[3,3,3,8,256]{4,3,2,1,0:T(8,128)(2,1)} %param.4) | copy-start | bytes 331780
  159.3 4.7 %slice-start = ((s8[4718592]{0:T(1024)(128)(4,1)}), s8[524288]{0:T(1024)(128)(4,1)S(1)}, s32[]{:S(2)}) async-start(s8[4718592]{0:T(1024)(128)(4,1)} %bitcast.383), calls=%async_computation.1 | async-start | bytes 1048576
  160.7 3.3 %slice-start.1 = ((s8[4718592]{0:T(1024)(128)(4,1)}), s8[4194304]{0:T(1024)(128)(4,1)S(1)}, s32[]{:S(2)}) async-start(s8[4718592]{0:T(1024)(128)(4,1)} %bitcast.383), calls=%async_computation.2 | async-start | bytes 8388608
Sparse Core Ops, SparseCore 0:
  19.9 112.1 all-gather.1
where the time goes:
time: 177 us; the launch traced here: 176 us
  waiting for transfers between devices  115 us (65%)
  matrix products  18.6 us (11%)
  local copies, waits for them, and re-layouts  13.8 us (8%)
  between operations  13.6 us (8%)
  other arithmetic  9.79 us (6%)
  starting transfers between devices  5.67 us (3%)
    all_gather x1, waiting for transfers between devices, body(): gathered = lax.all_gather(padded, 'filt', axis=1, tiled=True)  110 us
    dot_general x6, matrix products, convolve(): jnp.einsum('tc,cyx->tyx', flat_weight, volume_piece[plane_index], preferr...  18.6 us
    reshape x6, local copies, waits for them, and re-layouts, convolve(): products = products.reshape(depth_count, 3, 3, out_chan, in_rows, in_cols)  9.91 us
    add x2, other arithmetic, convolve(): totals[slot_index]  7.69 us
    ppermute x1, starting transfers between devices, with_halo(): before = lax.ppermute(last, axis, up)  4.38 us
    ppermute x1, waiting for transfers between devices, with_halo(): after = lax.ppermute(leading, axis, down)  4.18 us
  transfers between devices with their start and end apart: 3, of which 3 were waited for; matrix products, arithmetic and copies ran while one was open for 1% of the time, Pallas kernels for 0%

commit v1 on v0

--- a/solution.py
+++ b/solution.py
@@ -75,7 +75,15 @@
         bias_vector, lax.axis_index("filt") * own_count, own_count, 0
     )
     padded = with_halo(features, (("slab", 0),), 1)
-    gathered = lax.all_gather(padded, "filt", axis=1, tiled=True)
+    gathered = jnp.concatenate(
+        lax.all_to_all(
+            jnp.stack([padded for _ in range(lax.psum(1, axis_name="filt"))]),
+            axis_name="filt",
+            split_axis=0,
+            concat_axis=0,
+        ),
+        axis=1,
+    )
     convolved = convolve(gathered, kernel, 0, 1, planes)
     return finish(convolved, own_bias)
 

time: 177 us -> 398 us (2.25)
  the two profiles are of different devices: /device:TPU:1 before, /device:TPU:96 now
where the time goes in v1:
time: 398 us
  waiting for transfers between devices  328 us (82%)
  local copies, waits for them, and re-layouts  37.6 us (9%)
  starting transfers between devices  14.5 us (4%)
  matrix products  9.81 us (2%)
  other arithmetic  8.14 us (2%)
    all_to_all x1, waiting for transfers between devices, body(): lax.all_to_all(jnp.stack([padded for _ in range(lax.psum(1, axis_name='fi...  321 us
    slice x1, local copies, waits for them, and re-layouts, convolve(): volume_piece[plane_index]  17.2 us
    dot_general x6, matrix products, convolve(): jnp.einsum('tc,cyx->tyx', flat_weight, volume_piece[plane_index], preferr...  9.81 us
    another operation x1, local copies, waits for them, and re-layouts, body(): jnp.stack([padded for _ in range(lax.psum(1, axis_name='filt'))])  9.12 us
  transfers between devices with their start and end apart: 3, of which 3 were waited for; matrix products, arithmetic and copies ran while one was open for 0% of the time, Pallas kernels for 0%

profile of v1, /device:TPU:96, one launch (start us, length us, event | category | flops | bytes accessed | tf_op | source)
XLA Modules:
  0.0 397.7 jit_solution(12823796032234253907)
XLA Ops:
  0.0 1.0 fusion.160
  1.0 5.0 %collective-permute-start = (bf16[1,8,64,128]{3,2,1,0:T(8,128)(2,1)S(1)}, bf16[1,8,64,128]{3,2,1,0:T(8,128)(2,1)S(1)}, u32[]{:S(2)}, u32[]{:S(2)}) collective-permute-start(bf16[1,8,64,128]{3,2,1,0:T(8,128)(2,1)S(1)} %get-tuple-element.14), channel_id=1, source_target_pairs={{0,32},{32,64},{64,96},{96,128},{128,160},{160,192},{192,224},{1,3... | collective-permute-start | bytes 393224 | tf_op jit(solution)/shard_map/ppermute | solution.py:16
  6.0 1.9 collective-permute-start.1
  8.0 0.8 collective-permute-done
  8.8 5.3 %collective-permute-done.1 = bf16[1,8,64,128]{3,2,1,0:T(8,128)(2,1)S(1)} collective-permute-done((bf16[1,8,64,128]{3,2,1,0:T(8,128)(2,1)S(1)}, bf16[1,8,64,128]{3,2,1,0:T(8,128)(2,1)S(1)}, u32[]{:S(2)}, u32[]{:S(2)}) %collective-permute-start.1) | collective-permute-done | bytes 131104 | tf_op jit(solution)/shard_map/ppermute | solution.py:17
  14.1 1.1 pad_maximum_fusion
  15.8 9.1 %stack.4 = bf16[32,6,8,64,128]{4,2,3,1,0:T(8,128)(2,1)} broadcast(bf16[6,8,64,128]{3,1,2,0:T(8,128)(2,1)S(1)} %copy.23), dimensions={1,2,3,4} | broadcast | bytes 25952256 | tf_op jit(solution)/shard_map/stack | solution.py:80
  24.9 7.6 %all-to-all-start = ((bf16[32,6,8,64,128]{4,2,3,1,0:T(8,128)(2,1)}), bf16[32,6,8,64,128]{4,2,3,1,0:T(8,128)(2,1)}, u32[]{:S(2)}, u32[]{:S(2)}) async-start(bf16[32,6,8,64,128]{4,2,3,1,0:T(8,128)(2,1)} %stack.4), calls=%async_computation | async-start | bytes 50331648 | tf_op jit(solution)/shard_map/all_to_all | solution.py:79
  32.6 321.4 %all-to-all-done = bf16[32,6,8,64,128]{4,2,3,1,0:T(8,128)(2,1)} async-done(((bf16[32,6,8,64,128]{4,2,3,1,0:T(8,128)(2,1)}), bf16[32,6,8,64,128]{4,2,3,1,0:T(8,128)(2,1)}, u32[]{:S(2)}, u32[]{:S(2)}) %all-to-all-start) | async-done | bytes 25165856 | tf_op jit(solution)/shard_map/all_to_all | solution.py:79
  354.0 17.2 %fusion.159 = (bf16[1,32,8,64,128]{4,2,3,0,1:T(8,128)(2,1)}, bf16[1,32,8,64,128]{4,2,3,0,1:T(8,128)(2,1)}, bf16[1,32,8,64,128]{4,2,3,0,1:T(8,128)(2,1)}, bf16[1,...) fusion(bf16[6,32,8,64,128]{4,2,3,0,1:T(8,128)(2,1)} %bitcast), kind=kLoop, calls=%fused_computation.262 | loop fusion | bytes 50331648 | tf_op jit(solution)/shard_map/slice | solution.py:41
  371.2 3.3 fusion.6
  374.5 1.3 copy.31
  375.9 0.8 copy-done.1
  377.5 1.4 copy.28
  379.7 1.1 fusion.4
  380.8 1.3 copy.36
  382.1 3.0 fusion.2
  385.1 1.4 copy.41
  387.3 0.8 fusion
  388.6 0.9 copy-done.2
  389.5 0.8 fusion.10
  390.7 1.6 fusion.135
  392.4 4.3 %fusion.154 = (f32[1,8,64,128]{3,2,1,0:T(8,128)S(1)}, f32[1,8,64,128]{3,2,1,0:T(8,128)S(1)}, f32[1,8,64,128]{3,2,1,0:T(8,128)S(1)}) fusion(f32[3,3,3,8,64,128]{5,4,3,2,1,0:T(8,128)S(1)} %copy.36, f32[3,3,3,8,64,128]{5,4,3,2,1,0:T(8,128)S(1)} %copy.31, f32[2,3,3,8,64,128]{5,4,3,2,1,0:T(8,128)S(1)} %copy.28, f32[2,3,3,8,64,128]{5,4,3,2,1,0:T(8,128)S(1)} %copy.41, ...), kind=kLoop, calls=%fused_computation.253 | loop fusion | flops 5111808 | bytes 29097984 | tf_op jit(solution)/shard_map/add | solution.py:53
  396.7 1.0 fusion.18
  (17 shorter events, 3.8 us)
Async XLA Ops:
  1.0 7.8 %collective-permute-start = (bf16[1,8,64,128]{3,2,1,0:T(8,128)(2,1)S(1)}, bf16[1,8,64,128]{3,2,1,0:T(8,128)(2,1)S(1)}, u32[]{:S(2)}, u32[]{:S(2)}) collective-permute-start(bf16[1,8,64,128]{3,2,1,0:T(8,128)(2,1)S(1)} %get-tuple-element.14), channel_id=1, source_target_pairs={{0,32},{32,64},{64,96},{96,128},{128,160},{160,192},{192,224},{1,3... | collective-permute-start | bytes 393224 | tf_op jit(solution)/shard_map/ppermute | solution.py:16
  6.0 8.1 %collective-permute-start.1 = (bf16[1,8,64,128]{3,2,1,0:T(8,128)(2,1)S(1)}, bf16[1,8,64,128]{3,2,1,0:T(8,128)(2,1)S(1)}, u32[]{:S(2)}, u32[]{:S(2)}) collective-permute-start(bf16[1,8,64,128]{3,2,1,0:T(8,128)(2,1)S(1)} %get-tuple-element.15), channel_id=1, source_target_pairs={{32,0},{64,32},{96,64},{128,96},{160,128},{192,160},{224,192},{33,... | collective-permute-start | bytes 393224 | tf_op jit(solution)/shard_map/ppermute | solution.py:17
  24.9 7.6 %copy-start.5 = (f32[256]{0:T(256)S(1)}, f32[256]{0:T(256)}, u32[]{:S(2)}) copy-start(f32[256]{0:T(256)} %param.5) | copy-start | bytes 3076
  24.9 7.7 %copy-start.4 = (bf16[3,3,3,8,256]{4,3,2,1,0:T(8,128)(2,1)S(1)}, bf16[3,3,3,8,256]{4,3,2,1,0:T(8,128)(2,1)}, u32[]{:S(2)}) copy-start(bf16[3,3,3,8,256]{4,3,2,1,0:T(8,128)(2,1)} %param.4) | copy-start | bytes 331780
  24.9 329.1 %all-to-all-start = ((bf16[32,6,8,64,128]{4,2,3,1,0:T(8,128)(2,1)}), bf16[32,6,8,64,128]{4,2,3,1,0:T(8,128)(2,1)}, u32[]{:S(2)}, u32[]{:S(2)}) async-start(bf16[32,6,8,64,128]{4,2,3,1,0:T(8,128)(2,1)} %stack.4), calls=%async_computation | async-start | bytes 50331648 | tf_op jit(solution)/shard_map/all_to_all | solution.py:79
  374.5 2.2 copy-start.1
  377.5 2.2 copy-start
  385.1 2.2 copy-start.3
  387.3 2.2 copy-start.2
